TPU v7x, 32 devices: a whole 2x2x4 slice. The times are simulated.
32 devices in a mesh: space: 4 (over z), energy: 8 (over y, x, core).
Axes of the slice: x: 2, y: 2, z: 4, core: 2. Of those that a mesh axis runs over, the one named last changes fastest.
Arguments:
- retain: float32 [8, 8], P('space', 'energy'), may hold values from 0.12 to 0.89
- hopping: float32 [8, 8, 2, 128, 128], P('space', 'energy'), may hold values from -0.125 to 0.125
- source: float32 [8, 8, 2, 128, 128], P('space', 'energy'), may hold values from -0.9 to 0.9
- screened: float32 [8, 8, 2, 16384], P('space', None, None, 'energy'), may hold values from -2 to 2
Outputs:
- greens: float32 [8, 8, 2, 128, 128], P('space', 'energy')
- self_energy: float32 [8, 8, 2, 16384], P('space', None, None, 'energy')
All inputs are finite; a program needn't handle non-finite values.
Results may differ from a plain program's by a relative error of at most 0.0001.
Values sent between devices are 32-bit elements; how exact they have to be, the bound alone decides.
A program may use at most 64 MiB of HBM per device.

v0:
```python
import math

import jax
import jax.numpy as jnp
from jax import lax
from jax.sharding import PartitionSpec as P

EXACT_PRECISION = lax.Precision.HIGHEST


def shifted(value, axis, steps):
    count = lax.axis_size(axis)
    initial, last = (max(0, -steps), min(count, count - steps))
    return lax.ppermute(value, axis, [(source, source + steps) for source in range(initial, last)])


def build_coupler(retain_slab, hop_slab):
    size = hop_slab.shape[-1]
    diagonal_ones = jnp.eye(size, dtype=jnp.float32)
    factor = retain_slab[:, None, None]
    return jnp.stack([factor * (diagonal_ones + hop_slab[:, 0]), factor * hop_slab[:, 1]], axis=1)


def complex_product(left_matrix, right_matrix):
    real_component = jnp.einsum(
        "eij,ejk->eik", left_matrix[:, 0], right_matrix[:, 0], precision=EXACT_PRECISION
    ) - jnp.einsum("eij,ejk->eik", left_matrix[:, 1], right_matrix[:, 1], precision=EXACT_PRECISION)
    imaginary_component = jnp.einsum(
        "eij,ejk->eik", left_matrix[:, 0], right_matrix[:, 1], precision=EXACT_PRECISION
    ) + jnp.einsum("eij,ejk->eik", left_matrix[:, 1], right_matrix[:, 0], precision=EXACT_PRECISION)
    return jnp.stack([real_component, imaginary_component], axis=1)


def times_dagger(left_matrix, right_matrix):
    real_component = jnp.einsum(
        "eij,ekj->eik", left_matrix[:, 0], right_matrix[:, 0], precision=EXACT_PRECISION
    ) + jnp.einsum("eij,ekj->eik", left_matrix[:, 1], right_matrix[:, 1], precision=EXACT_PRECISION)
    imaginary_component = jnp.einsum(
        "eij,ekj->eik", left_matrix[:, 1], right_matrix[:, 0], precision=EXACT_PRECISION
    ) - jnp.einsum("eij,ekj->eik", left_matrix[:, 0], right_matrix[:, 1], precision=EXACT_PRECISION)
    return jnp.stack([real_component, imaginary_component], axis=1)


def sandwich(coupler, middle):
    return times_dagger(complex_product(coupler, middle), coupler)


def fourier_tables(length, columns):
    rows_index = jnp.arange(length, dtype=jnp.int32)[:, None]
    cols_index = jnp.arange(columns, dtype=jnp.int32)[None, :]
    phases = (rows_index * cols_index % length).astype(jnp.float32) * (2.0 * math.pi / length)
    return (jnp.cos(phases), jnp.sin(phases))


def forward_transform(series, cosine_lookup, sine_lookup):
    real_input = series[:, :, 0]
    imaginary_input = series[:, :, 1]
    real_component = jnp.einsum(
        "gt,itx->igx", cosine_lookup, real_input, precision=EXACT_PRECISION
    ) + jnp.einsum("gt,itx->igx", sine_lookup, imaginary_input, precision=EXACT_PRECISION)
    imaginary_component = jnp.einsum(
        "gt,itx->igx", cosine_lookup, imaginary_input, precision=EXACT_PRECISION
    ) - jnp.einsum("gt,itx->igx", sine_lookup, real_input, precision=EXACT_PRECISION)
    return jnp.stack([real_component, imaginary_component], axis=2)


def body(retain, hopping, source, screened):
    couplers = jax.vmap(build_coupler)(retain, hopping)

    def compose_step(running, slab_data):
        total_map, total_source = running
        coupler, fresh_source = slab_data
        return (
            (complex_product(coupler, total_map), sandwich(coupler, total_source) + fresh_source),
            None,
        )

    (device_map, device_source), _ = lax.scan(
        compose_step, (couplers[0], source[0]), (couplers[1:], source[1:])
    )

    def hand_over(counter, arriving):
        leaving = sandwich(device_map, arriving) + device_source
        return shifted(leaving, "space", 1)

    entering = lax.fori_loop(
        0, lax.axis_size("space") - 1, hand_over, jnp.zeros_like(device_source)
    )

    def apply_step(arriving, slab_data):
        coupler, fresh_source = slab_data
        leaving = sandwich(coupler, arriving) + fresh_source
        return (leaving, leaving)

    _, greens = lax.scan(apply_step, entering, (couplers, source))
    pair_blocks = greens.reshape(
        greens.shape[0], greens.shape[1], 2, greens.shape[3] * greens.shape[4]
    )
    total_energies = greens.shape[1] * lax.axis_size("energy")
    period = 2 * total_energies
    cosine_lookup, sine_lookup = fourier_tables(period, total_energies)
    green_spectrum = forward_transform(
        lax.all_to_all(pair_blocks, "energy", split_axis=3, concat_axis=1, tiled=True),
        cosine_lookup,
        sine_lookup,
    )
    screen_spectrum = forward_transform(screened, cosine_lookup, sine_lookup)
    real_result = (
        green_spectrum[:, :, 0] * screen_spectrum[:, :, 0]
        - green_spectrum[:, :, 1] * screen_spectrum[:, :, 1]
    )
    imaginary_result = (
        green_spectrum[:, :, 0] * screen_spectrum[:, :, 1]
        + green_spectrum[:, :, 1] * screen_spectrum[:, :, 0]
    )
    real_component = (
        jnp.einsum("wo,cwd->cod", cosine_lookup, real_result, precision=EXACT_PRECISION)
        - jnp.einsum("wo,cwd->cod", sine_lookup, imaginary_result, precision=EXACT_PRECISION)
    ) / period
    imaginary_component = (
        jnp.einsum("wo,cwd->cod", cosine_lookup, imaginary_result, precision=EXACT_PRECISION)
        + jnp.einsum("wo,cwd->cod", sine_lookup, real_result, precision=EXACT_PRECISION)
    ) / period
    self_energy = jnp.stack([real_component, imaginary_component], axis=2)
    return (greens, self_energy)


def solution(mesh):
    placed = (
        P("space", "energy"),
        P("space", "energy", None, None, None),
        P("space", "energy", None, None, None),
        P("space", None, None, "energy"),
    )
    return jax.shard_map(
        body,
        mesh=mesh,
        in_specs=placed,
        out_specs=(P("space", "energy", None, None, None), P("space", None, None, "energy")),
        check_vma=False,
    )
```

profile of v0, /device:TPU:25, one launch (start us, length us, event | category | flops | bytes accessed | tf_op | source)
XLA Modules:
  0.0 139.5 jit_solution(247373426349361048)
XLA Ops:
  0.6 1.1 slice_multiply_fusion
  1.7 0.9 fusion.56
  4.5 0.3 fusion.52
  4.8 0.3 fusion.51
  5.5 0.9 maximum_add_fusion.3
  6.4 23.6 %while.8 = (s32[]{:T(128)}, f32[1,2,128,128]{3,2,1,0:T(8,128)S(1)}, f32[1,2,128,128]{3,2,1,0:T(8,128)S(1)}, f32[1,2,128,128]{3,2,1,0:T(8,128)S(1)}, s32[]{:T(128)}) while((s32[]{:T(128)}, f32[1,2,128,128]{3,2,1,0:T(8,128)S(1)}, f32[1,2,128,128]{3,2,1,0:T(8,128)S(1)}, f32[1,2,128,128]{3,2,1,0:T(8,128)S(1)}, s32[]{:T(128)}) %tuple.44), condition=%wide.region_1.2_spmd, body=%wide.region_0.1_spmd.sunk | while | flops 201457664 | bytes 2752613 | solution.py:86
  7.8 0.3 fusion.223
  8.1 0.3 fusion.225
  8.4 1.3 collective-permute-start
  9.7 5.0 %collective-permute-done = f32[1,2,128,128]{3,2,1,0:T(8,128)S(1)} collective-permute-done((f32[1,2,128,128]{3,2,1,0:T(8,128)S(1)}, f32[1,2,128,128]{3,2,1,0:T(8,128)S(1)}, u32[]{:S(2)}, u32[]{:S(2)}) %collective-permute-start) | collective-permute-done | bytes 131104 | tf_op jit(solution)/shard_map/while/body/eval_jaxpr/ppermute | solution.py:14
  16.1 0.3 fusion.223
  16.3 0.3 fusion.225
  16.6 1.3 collective-permute-start
  17.9 4.4 %collective-permute-done = f32[1,2,128,128]{3,2,1,0:T(8,128)S(1)} collective-permute-done((f32[1,2,128,128]{3,2,1,0:T(8,128)S(1)}, f32[1,2,128,128]{3,2,1,0:T(8,128)S(1)}, u32[]{:S(2)}, u32[]{:S(2)}) %collective-permute-start) | collective-permute-done | bytes 131104 | tf_op jit(solution)/shard_map/while/body/eval_jaxpr/ppermute | solution.py:14
  23.7 0.3 fusion.223
  24.0 0.3 fusion.225
  24.3 1.3 collective-permute-start
  25.6 4.4 %collective-permute-done = f32[1,2,128,128]{3,2,1,0:T(8,128)S(1)} collective-permute-done((f32[1,2,128,128]{3,2,1,0:T(8,128)S(1)}, f32[1,2,128,128]{3,2,1,0:T(8,128)S(1)}, u32[]{:S(2)}, u32[]{:S(2)}) %collective-permute-start) | collective-permute-done | bytes 131104 | tf_op jit(solution)/shard_map/while/body/eval_jaxpr/ppermute | solution.py:14
  30.0 7.6 %while.28 = (s32[]{:T(128)}, f32[1,2,128,128]{3,2,1,0:T(8,128)S(1)}, f32[2,1,2,128,128]{4,3,2,1,0:T(8,128)S(1)}, f32[2,1,2,128,128]{4,3,2,1,0:T(8,128)S(1)}, f32[2,1,2,128,128]{4,3,2,1,0:T(8,128)}, /*index=5*/s32[]{:T(128)}) while((s32[]{:T(128)}, f32[1,2,128,128]{3,2,1,0:T(8,128)S(1)}, f32[2,1,2,128,128]{4,3,2,1,0:T(8,128)S(1)}, ...), condition=%wide.region_3.4_spmd, body=%wide.region_2.3_spmd.sunk | while | flops 201523200 | bytes 2883665 | solution.py:95
  31.4 0.3 fusion.235
  31.7 0.3 convolution_subtract_fusion.15
  31.9 0.9 fusion.238
  32.9 0.9 maximum_add_fusion.7
  35.2 0.3 fusion.235
  35.5 0.3 convolution_subtract_fusion.15
  35.8 0.9 fusion.238
  36.7 0.9 maximum_add_fusion.7
  37.6 11.3 %copy.10 = f32[2,1,2,128,128]{0,2,4,3,1:T(2,128)} copy(f32[2,1,2,128,128]{4,3,2,1,0:T(8,128)S(1)} %get-tuple-element.70) | data formatting | bytes 524288 | tf_op jit(solution)/shard_map/while | solution.py:95
  49.0 25.8 %reshape.358 = f32[8,1,8192]{2,1,0:T(1,128)} reshape(f32[16384,1,2,2]{3,2,1,0:T(2,128)} %bitcast.277) | data formatting | bytes 524288
  74.8 7.5 %all-to-all-start = ((f32[8,1,8192]{2,1,0:T(1,128)}), f32[8,1,8192]{2,1,0:T(1,128)S(1)}, u32[]{:S(2)}, u32[]{:S(2)}) async-start(f32[8,1,8192]{2,1,0:T(1,128)} %reshape.358), calls=%async_computation | async-start | bytes 524288 | tf_op jit(solution)/shard_map/all_to_all | solution.py:103
  82.6 0.5 fusion.60
  83.0 0.5 fusion.59
  83.5 0.5 fusion.43
  84.0 0.5 fusion.45
  84.5 3.6 %all-to-all-done = f32[8,1,8192]{2,1,0:T(1,128)S(1)} async-done(((f32[8,1,8192]{2,1,0:T(1,128)}), f32[8,1,8192]{2,1,0:T(1,128)S(1)}, u32[]{:S(2)}, u32[]{:S(2)}) %all-to-all-start) | async-done | bytes 262176 | tf_op jit(solution)/shard_map/all_to_all | solution.py:103
  88.0 0.5 broadcast.72
  88.5 1.3 reduce
  89.8 32.2 %reshape.359 = f32[16384,1,2,2]{3,2,1,0:T(2,128)} reshape(f32[8,8192]{1,0:T(8,128)S(1)} %reduce) | data formatting | bytes 524288
  122.0 13.4 %copy.15 = f32[2,1,2,8,2048]{4,3,0,2,1:T(8,128)S(1)} copy(f32[2,1,2,8,2048]{0,2,4,3,1:T(2,128)} %bitcast.276) | data formatting | bytes 524288 | tf_op jit(solution)/shard_map/all_to_all | solution.py:103
  135.4 0.5 fusion.61
  135.8 0.5 fusion.62
  136.3 0.5 fusion.46
  136.8 0.5 multiply_subtract_fusion
  137.3 0.3 fusion.81
  137.6 0.3 fusion.79
  137.9 0.3 fusion.50
  138.2 0.3 fusion.48
  138.6 0.9 copy.14
  (56 shorter events, 9.3 us)
Async XLA Ops:
  8.4 6.3 %collective-permute-start = (f32[1,2,128,128]{3,2,1,0:T(8,128)S(1)}, f32[1,2,128,128]{3,2,1,0:T(8,128)S(1)}, u32[]{:S(2)}, u32[]{:S(2)}) collective-permute-start(f32[1,2,128,128]{3,2,1,0:T(8,128)S(1)} %maximum_add_fusion.6), channel_id=1, source_target_pairs={{0,8},{8,16},{16,24},{1,9},{9,17},{17,25},{2,10},{10,18},{18,26},{... | collective-permute-start | bytes 393224 | tf_op jit(solution)/shard_map/while/body/eval_jaxpr/ppermute | solution.py:14
  16.6 5.7 %collective-permute-start = (f32[1,2,128,128]{3,2,1,0:T(8,128)S(1)}, f32[1,2,128,128]{3,2,1,0:T(8,128)S(1)}, u32[]{:S(2)}, u32[]{:S(2)}) collective-permute-start(f32[1,2,128,128]{3,2,1,0:T(8,128)S(1)} %maximum_add_fusion.6), channel_id=1, source_target_pairs={{0,8},{8,16},{16,24},{1,9},{9,17},{17,25},{2,10},{10,18},{18,26},{... | collective-permute-start | bytes 393224 | tf_op jit(solution)/shard_map/while/body/eval_jaxpr/ppermute | solution.py:14
  24.3 5.7 %collective-permute-start = (f32[1,2,128,128]{3,2,1,0:T(8,128)S(1)}, f32[1,2,128,128]{3,2,1,0:T(8,128)S(1)}, u32[]{:S(2)}, u32[]{:S(2)}) collective-permute-start(f32[1,2,128,128]{3,2,1,0:T(8,128)S(1)} %maximum_add_fusion.6), channel_id=1, source_target_pairs={{0,8},{8,16},{16,24},{1,9},{9,17},{17,25},{2,10},{10,18},{18,26},{... | collective-permute-start | bytes 393224 | tf_op jit(solution)/shard_map/while/body/eval_jaxpr/ppermute | solution.py:14
  37.6 37.2 %copy-start = (f32[2,1,2,128,128]{4,3,2,1,0:T(8,128)}, f32[2,1,2,128,128]{4,3,2,1,0:T(8,128)S(1)}, u32[]{:S(2)}) copy-start(f32[2,1,2,128,128]{4,3,2,1,0:T(8,128)S(1)} %get-tuple-element.70) | copy-start | bytes 786436
  37.6 44.7 %copy-start.1 = (f32[2,8,2,2048]{3,2,1,0:T(2,128)S(1)}, f32[2,8,2,2048]{3,2,1,0:T(2,128)}, u32[]{:S(2)}) copy-start(f32[2,8,2,2048]{3,2,1,0:T(2,128)} %param.11) | copy-start | bytes 786436
  74.8 13.2 %all-to-all-start = ((f32[8,1,8192]{2,1,0:T(1,128)}), f32[8,1,8192]{2,1,0:T(1,128)S(1)}, u32[]{:S(2)}, u32[]{:S(2)}) async-start(f32[8,1,8192]{2,1,0:T(1,128)} %reshape.358), calls=%async_computation | async-start | bytes 524288 | tf_op jit(solution)/shard_map/all_to_all | solution.py:103
where the time goes:
time: 141 us; the launch traced here: 139 us
  local copies, waits for them, and re-layouts  84.4 us (60%)
  waiting for transfers between devices  17.3 us (12%)
  matrix products  17.2 us (12%)
  starting transfers between devices  11.4 us (8%)
  other arithmetic  7.99 us (6%)
    unnamed x7, local copies, waits for them, and re-layouts  58.9 us
    all_to_all x2, local copies, waits for them, and re-layouts, body(): lax.all_to_all(pair_blocks, 'energy', split_axis=3, concat_axis=1, tiled=...  13.9 us
    ppermute x3, waiting for transfers between devices, shifted(): lax.ppermute(value, axis, [(source, source + steps) for source in range(i...  13.8 us
    while x1, local copies, waits for them, and re-layouts, body(): _, greens = lax.scan(apply_step, entering, (couplers, source))  11.3 us
    all_to_all x1, starting transfers between devices, body(): lax.all_to_all(pair_blocks, 'energy', split_axis=3, concat_axis=1, tiled=...  7.54 us
    ppermute x3, starting transfers between devices, shifted(): lax.ppermute(value, axis, [(source, source + steps) for source in range(i...  3.88 us
    all_to_all x1, waiting for transfers between devices, body(): lax.all_to_all(pair_blocks, 'energy', split_axis=3, concat_axis=1, tiled=...  3.56 us
  transfers between devices with their start and end apart: 4, of which 4 were waited for; matrix products, arithmetic and copies ran while one was open for 1% of the time, Pallas kernels for 0%

commit v1 on v0

v1 whole, which is shorter than its diff:
```python
import functools

import jax
import jax.numpy as jnp
from jax import lax
from jax.experimental import pallas as pl
from jax.experimental.pallas import tpu as pltpu
from jax.sharding import PartitionSpec as P

MESH = pl.DeviceIdType.MESH
F32 = jnp.float32
BF16 = jnp.bfloat16
CHUNKS = 2
NN = (((1,), (0,)), ((), ()))
NT = (((1,), (1,)), ((), ()))


def split(value):
    high = value.astype(BF16)
    return high, (value - high.astype(F32)).astype(BF16)


def product(left, right, dims=NN):
    dot = functools.partial(lax.dot_general, dimension_numbers=dims, preferred_element_type=F32)
    (lh, ll), (rh, rl) = left, right
    return dot(lh, rh) + (dot(lh, rl) + dot(ll, rh))


def left_form(real, imag):
    return jnp.concatenate(
        [jnp.concatenate([real, -imag], 1), jnp.concatenate([imag, real], 1)], 0
    )


def dagger_form(real, imag):
    return jnp.concatenate(
        [jnp.concatenate([real, imag], 1), jnp.concatenate([-imag, real], 1)], 0
    )


def kernel(
    retain, hop_hbm, src_hbm, scr_hbm, out_g, out_se,
    hop, src, scr, lefts, rights, bases, g, stage, entering, landed,
    load_sem, chain_send, chain_recv, swap_send, swap_recv, out_sem,
):
    slabs, _, size, _ = hop.shape
    energies, rows = stage.shape[1], stage.shape[3]
    space, energy = lax.axis_index("space"), lax.axis_index("energy")
    stages = lax.axis_size("space")
    piece = size // CHUNKS

    loads = [
        pltpu.make_async_copy(hop_hbm.at[:, 0], hop, load_sem.at[0]),
        pltpu.make_async_copy(src_hbm.at[:, 0], src, load_sem.at[1]),
        pltpu.make_async_copy(scr_hbm, scr, load_sem.at[2]),
    ]
    for load in loads:
        load.start()

    barrier = pltpu.get_barrier_semaphore()
    for step in range(1, energies):
        pl.semaphore_signal(
            barrier, inc=1, device_id=(space, lax.rem(energy + step, energies)), device_id_type=MESH
        )

    @pl.when(space > 0)
    def _():
        pl.semaphore_signal(barrier, inc=1, device_id=(space - 1, energy), device_id_type=MESH)

    loads[0].wait()
    loads[1].wait()

    eye = (
        lax.broadcasted_iota(jnp.int32, (size, size), 0)
        == lax.broadcasted_iota(jnp.int32, (size, size), 1)
    ).astype(F32)
    couplers = []
    for j in range(slabs):
        factor = retain[j, 0]
        couplers.append((factor * (eye + hop[j, 0]), factor * hop[j, 1]))

    def sandwich(left, right, real, imag):
        turned = product(split(jnp.concatenate([real, imag], 1)), right, NT)
        return product(left, split(jnp.concatenate([turned[:, :size], turned[:, size:]], 0)))

    base = jnp.concatenate([src[0, 0], src[0, 1]], 0)
    bases[0] = base
    step_lefts = [None]
    for j in range(1, slabs):
        step_left = split(left_form(*couplers[j]))
        step_right = split(dagger_form(*couplers[j]))
        step_lefts.append(step_left)
        base = sandwich(step_left, step_right, base[:size], base[size:]) + jnp.concatenate(
            [src[j, 0], src[j, 1]], 0
        )
        bases[j] = base

    def chain(c):
        part = pl.ds(c * piece, piece)
        return pltpu.make_async_remote_copy(
            src_ref=g.at[slabs - 1, :, part],
            dst_ref=entering.at[:, part],
            send_sem=chain_send.at[c],
            recv_sem=chain_recv.at[c],
            device_id=(space + 1, energy),
            device_id_type=MESH,
        )

    def swap(j, step):
        peer = lax.rem(energy + step, energies)
        return pltpu.make_async_remote_copy(
            src_ref=stage.at[j, peer],
            dst_ref=landed.at[j, energy],
            send_sem=swap_send.at[j, step],
            recv_sem=swap_recv.at[j, step],
            device_id=(space, peer),
            device_id_type=MESH,
        )

    def put(j, block):
        g[j, 0] = block[:size]
        g[j, 1] = block[size:]

    def spread(j):
        for q in range(energies):
            for part in range(2):
                stage[j, q, part] = g[j, part, q * rows : (q + 1) * rows]
        for step in range(1, energies):
            swap(j, step).start()
        pltpu.make_async_copy(g.at[j], out_g.at[j, 0], out_sem.at[j]).start()

    pl.semaphore_wait(barrier, energies - 1 + (space < stages - 1).astype(jnp.int32))

    last = slabs - 1

    @pl.when(space == 0)
    def _():
        put(last, bases[last])

        @pl.when(space < stages - 1)
        def _():
            for c in range(CHUNKS):
                chain(c).start()

        spread(last)
        for j in range(last - 1, -1, -1):
            put(j, bases[j])
            spread(j)

    @pl.when(space > 0)
    def _():
        real, imag = couplers[0]
        for j in range(slabs):
            if j > 0:
                both = product(step_lefts[j], split(jnp.concatenate([real, imag], 0)))
                real, imag = both[:size], both[size:]
            for ref, form in ((lefts, left_form), (rights, dagger_form)):
                high, low = split(form(real, imag))
                ref[j, 0] = high
                ref[j, 1] = low

        turned = []
        for c in range(CHUNKS):
            chain(c).wait_recv()
            lines = slice(c * piece, (c + 1) * piece)
            arrived = split(jnp.concatenate([entering[0, lines], entering[1, lines]], 1))
            turned.append(product(arrived, (rights[last, 0], rights[last, 1]), NT))
        turned = jnp.concatenate(turned, 0)
        inner = split(jnp.concatenate([turned[:, :size], turned[:, size:]], 0))
        put(last, product((lefts[last, 0], lefts[last, 1]), inner) + bases[last])

        @pl.when(space < stages - 1)
        def _():
            for c in range(CHUNKS):
                chain(c).start()

        spread(last)
        for j in range(last - 1, -1, -1):
            put(
                j,
                sandwich(
                    (lefts[j, 0], lefts[j, 1]),
                    (rights[j, 0], rights[j, 1]),
                    entering[0],
                    entering[1],
                )
                + bases[j],
            )
            spread(j)

    loads[2].wait()
    for j in range(last, -1, -1):
        landed[j, energy] = stage[j, energy]
        for step in range(1, energies):
            swap(j, step).wait_recv()
        for e in range(energies):
            real = jnp.zeros((rows, size), F32)
            imag = jnp.zeros((rows, size), F32)
            for w in range(e + 1):
                gr, gi = landed[j, e - w, 0], landed[j, e - w, 1]
                sr, si = scr[j, w, 0], scr[j, w, 1]
                real = real + (gr * sr - gi * si)
                imag = imag + (gr * si + gi * sr)
            out_se[j, e, 0] = real
            out_se[j, e, 1] = imag

    for j in range(slabs):
        for step in range(1, energies):
            swap(j, step).wait_send()
        pltpu.make_async_copy(g.at[j], out_g.at[j, 0], out_sem.at[j]).wait()

    @pl.when(space < stages - 1)
    def _():
        for c in range(CHUNKS):
            chain(c).wait_send()


def body(retain, hopping, source, screened):
    slabs, _, _, size, _ = hopping.shape
    energies = screened.shape[1]
    rows = screened.shape[3] // size
    tall = screened.reshape(slabs, energies, 2, rows, size)
    any_spec = pl.BlockSpec(memory_space=pl.ANY)
    vmem = pltpu.VMEM
    greens, self_energy = pl.pallas_call(
        kernel,
        out_shape=(
            jax.ShapeDtypeStruct(source.shape, F32),
            jax.ShapeDtypeStruct(tall.shape, F32),
        ),
        in_specs=[pl.BlockSpec(memory_space=pltpu.SMEM), any_spec, any_spec, any_spec],
        out_specs=(any_spec, pl.BlockSpec(memory_space=pltpu.VMEM)),
        scratch_shapes=[
            vmem((slabs, 2, size, size), F32),
            vmem((slabs, 2, size, size), F32),
            vmem(tall.shape, F32),
            vmem((slabs, 2, 2 * size, 2 * size), BF16),
            vmem((slabs, 2, 2 * size, 2 * size), BF16),
            vmem((slabs, 2 * size, size), F32),
            vmem((slabs, 2, size, size), F32),
            vmem((slabs, energies, 2, rows, size), F32),
            vmem((2, size, size), F32),
            vmem((slabs, energies, 2, rows, size), F32),
            pltpu.SemaphoreType.DMA((3,)),
            pltpu.SemaphoreType.DMA((CHUNKS,)),
            pltpu.SemaphoreType.DMA((CHUNKS,)),
            pltpu.SemaphoreType.DMA((slabs, energies)),
            pltpu.SemaphoreType.DMA((slabs, energies)),
            pltpu.SemaphoreType.DMA((slabs,)),
        ],
        compiler_params=pltpu.CompilerParams(collective_id=0, has_side_effects=True),
    )(retain, hopping, source, tall)
    return greens, self_energy.reshape(screened.shape)


def solution(mesh):
    placed = (
        P("space", "energy"),
        P("space", "energy", None, None, None),
        P("space", "energy", None, None, None),
        P("space", None, None, "energy"),
    )
    return jax.shard_map(
        body,
        mesh=mesh,
        in_specs=placed,
        out_specs=(P("space", "energy", None, None, None), P("space", None, None, "energy")),
        check_vma=False,
    )
```

time: 141 us -> 27.8 us (0.20)
  local copies, waits for them, and re-layouts: 84.4 us -> 5.69 us
  Pallas kernels: 0 us -> 21.2 us
  waiting for transfers between devices: 17.3 us -> 0 us
  matrix products: 17.2 us -> 0 us
  starting transfers between devices: 11.4 us -> 0 us
  other arithmetic: 7.99 us -> 0 us
    unnamed x7 -> x4, local copies, waits for them, and re-layouts: 58.9 us -> 2 us
    pallas_call x0 -> x1, Pallas kernels: none -> 21.2 us  [body(): pl.pallas_call(kernel, out_shape=(jax.ShapeDtypeStruct(source.shape, F32)...]
    dot_general x64 -> x0, matrix products: 17.2 us -> none  [the longest x6 1.62 us: times_dagger(): jnp.einsum('eij,ekj->eik', left_matrix[:, 0], right_matrix[:, 1], precisi...]
    all_to_all x2 -> x0, local copies, waits for them, and re-layouts: 13.9 us -> none  [body(): lax.all_to_all(pair_blocks, 'energy', split_axis=3, concat_axis=1, tiled=...]
    ppermute x3 -> x0, waiting for transfers between devices: 13.8 us -> none  [shifted(): lax.ppermute(value, axis, [(source, source + steps) for source in range(i...]
    while x1 -> x0, local copies, waits for them, and re-layouts: 11.3 us -> none  [body(): _, greens = lax.scan(apply_step, entering, (couplers, source))]
    all_to_all x1 -> x0, starting transfers between devices: 7.54 us -> none  [body(): lax.all_to_all(pair_blocks, 'energy', split_axis=3, concat_axis=1, tiled=...]
    ppermute x3 -> x0, starting transfers between devices: 3.88 us -> none  [shifted(): lax.ppermute(value, axis, [(source, source + steps) for source in range(i...]
  transfers between devices with their start and end apart: 4 -> 0, of which waited for: 4 -> 0; matrix products, arithmetic and copies ran while one was open for 1% -> 0% of each run, Pallas kernels for 0% -> 0%
where the time goes in v1:
time: 27.8 us; the launch traced here: 27.6 us
  Pallas kernels  21.2 us (76%)
  local copies, waits for them, and re-layouts  5.69 us (20%)
  between operations  0.65 us (2%)
    pallas_call x1, Pallas kernels, body(): pl.pallas_call(kernel, out_shape=(jax.ShapeDtypeStruct(source.shape, F32)...  21.2 us
    unnamed x4, local copies, waits for them, and re-layouts  2 us
    reshape x1, local copies, waits for them, and re-layouts, body(): tall = screened.reshape(slabs, energies, 2, rows, size)  1.86 us
    reshape x1, local copies, waits for them, and re-layouts, body(): return (greens, self_energy.reshape(screened.shape))  1.83 us

profile of v1, /device:TPU:25, one launch (start us, length us, event | category | flops | bytes accessed | tf_op | source)
XLA Modules:
  0.0 27.6 jit_solution(709707981588834322)
XLA Ops:
  0.6 1.3 %copy.6.retain = f32[2,1]{1,0:T(2,128)} copy(f32[2,1]{0,1:T(1,128)} %param.4) | data formatting | bytes 16 | tf_op args[0]
  1.9 1.9 %reshape.10.scr_hbm = f32[2,8,2,16,128]{4,3,2,1,0:T(8,128)} reshape(f32[2,8,2,2048]{3,2,1,0:T(2,128)} %param.7) | data formatting | bytes 524288 | tf_op jit(solution)/shard_map/reshape | solution.py:222
  3.8 21.2 %shard_map.59 = (f32[2,1,2,128,128]{4,3,2,1,0:T(8,128)}, f32[2,8,2,16,128]{4,3,2,1,0:T(8,128)}) custom-call(f32[2,1]{1,0:T(2,128)} %copy.6.retain, f32[2,1,2,128,128]{4,3,2,1,0:T(8,128)} %hop_hbm.1, f32[2,1,2,128,128]{4,3,2,1,0:T(8,128)} %src_hbm.1, f32[2,8,2,16,128]{4,3,2,1,0:T(8,128)} %reshape.10.scr_hbm), custom_call_target="tpu_custom_call" | custom-call | tf_op jit(solution)/shard_map/pallas_call | solution.py:225
  25.0 0.0 copy-start
  25.0 1.8 %reshape.11 = f32[2,8,2,2048]{3,2,1,0:T(2,128)} reshape(f32[2,8,2,16,128]{4,3,2,1,0:T(8,128)} %get-tuple-element.5) | data formatting | bytes 524288 | tf_op jit(solution)/shard_map/reshape | solution.py:253
  26.8 0.0 copy-done
  26.9 0.7 %copy.8 = f32[2,1,2,128,128]{4,3,2,1,0:T(8,128)} copy(f32[2,1,2,128,128]{4,3,2,1,0:T(8,128)S(1)} %copy-done) | data formatting | bytes 524288
Async XLA Ops:
  25.0 1.8 %copy-start = (f32[2,1,2,128,128]{4,3,2,1,0:T(8,128)S(1)}, f32[2,1,2,128,128]{4,3,2,1,0:T(8,128)}, u32[]{:S(2)}) copy-start(f32[2,1,2,128,128]{4,3,2,1,0:T(8,128)} %get-tuple-element.8) | copy-start | bytes 786436

commit v2 on v1

--- a/solution.py
+++ b/solution.py
@@ -39,9 +39,9 @@
 
 
 def kernel(
-    retain, hop_hbm, src_hbm, scr_hbm, out_g, out_se,
-    hop, src, scr, lefts, rights, bases, g, stage, entering, landed,
-    load_sem, chain_send, chain_recv, swap_send, swap_recv, out_sem,
+    retain_hbm, hop_hbm, src_hbm, scr_hbm, g, out_se,
+    retain, hop, src, scr, lefts, rights, bases, stage, entering, landed,
+    load_sem, chain_send, chain_recv, swap_send, swap_recv,
 ):
     slabs, _, size, _ = hop.shape
     energies, rows = stage.shape[1], stage.shape[3]
@@ -53,6 +53,7 @@
         pltpu.make_async_copy(hop_hbm.at[:, 0], hop, load_sem.at[0]),
         pltpu.make_async_copy(src_hbm.at[:, 0], src, load_sem.at[1]),
         pltpu.make_async_copy(scr_hbm, scr, load_sem.at[2]),
+        pltpu.make_async_copy(retain_hbm, retain, load_sem.at[3]),
     ]
     for load in loads:
         load.start()
@@ -67,6 +68,7 @@
     def _():
         pl.semaphore_signal(barrier, inc=1, device_id=(space - 1, energy), device_id_type=MESH)
 
+    loads[3].wait()
     loads[0].wait()
     loads[1].wait()
 
@@ -76,7 +78,7 @@
     ).astype(F32)
     couplers = []
     for j in range(slabs):
-        factor = retain[j, 0]
+        factor = retain[j]
         couplers.append((factor * (eye + hop[j, 0]), factor * hop[j, 1]))
 
     def sandwich(left, right, real, imag):
@@ -127,7 +129,6 @@
                 stage[j, q, part] = g[j, part, q * rows : (q + 1) * rows]
         for step in range(1, energies):
             swap(j, step).start()
-        pltpu.make_async_copy(g.at[j], out_g.at[j, 0], out_sem.at[j]).start()
 
     pl.semaphore_wait(barrier, energies - 1 + (space < stages - 1).astype(jnp.int32))
 
@@ -188,6 +189,9 @@
             )
             spread(j)
 
+    def lanes(part):
+        return pl.ds(part, rows, stride=2)
+
     loads[2].wait()
     for j in range(last, -1, -1):
         landed[j, energy] = stage[j, energy]
@@ -198,16 +202,15 @@
             imag = jnp.zeros((rows, size), F32)
             for w in range(e + 1):
                 gr, gi = landed[j, e - w, 0], landed[j, e - w, 1]
-                sr, si = scr[j, w, 0], scr[j, w, 1]
+                sr, si = scr[j, w, lanes(0)], scr[j, w, lanes(1)]
                 real = real + (gr * sr - gi * si)
                 imag = imag + (gr * si + gi * sr)
-            out_se[j, e, 0] = real
-            out_se[j, e, 1] = imag
+            out_se[j, e, lanes(0)] = real
+            out_se[j, e, lanes(1)] = imag
 
     for j in range(slabs):
         for step in range(1, energies):
             swap(j, step).wait_send()
-        pltpu.make_async_copy(g.at[j], out_g.at[j, 0], out_sem.at[j]).wait()
 
     @pl.when(space < stages - 1)
     def _():
@@ -215,42 +218,71 @@
             chain(c).wait_send()
 
 
+def write_out(g, se, out_g, out_se, sems):
+    copies = [
+        pltpu.make_async_copy(g, out_g.at[:, 0], sems.at[0]),
+        pltpu.make_async_copy(se, out_se, sems.at[1]),
+    ]
+    for copy in copies:
+        copy.start()
+    for copy in copies:
+        copy.wait()
+
+
 def body(retain, hopping, source, screened):
     slabs, _, _, size, _ = hopping.shape
     energies = screened.shape[1]
     rows = screened.shape[3] // size
-    tall = screened.reshape(slabs, energies, 2, rows, size)
+    woven = (
+        screened.reshape(slabs, energies, 2, rows, size)
+        .transpose(0, 1, 3, 2, 4)
+        .reshape(slabs, energies, 2 * rows, size)
+    )
     any_spec = pl.BlockSpec(memory_space=pl.ANY)
+    vmem_spec = pl.BlockSpec(memory_space=pltpu.VMEM)
     vmem = pltpu.VMEM
     greens, self_energy = pl.pallas_call(
         kernel,
-        out_shape=(
-            jax.ShapeDtypeStruct(source.shape, F32),
-            jax.ShapeDtypeStruct(tall.shape, F32),
-        ),
-        in_specs=[pl.BlockSpec(memory_space=pltpu.SMEM), any_spec, any_spec, any_spec],
-        out_specs=(any_spec, pl.BlockSpec(memory_space=pltpu.VMEM)),
+        out_shape=(vmem((slabs, 2, size, size), F32), vmem(woven.shape, F32)),
+        in_specs=[pl.BlockSpec(memory_space=pltpu.HBM)] * 4,
+        out_specs=(vmem_spec, vmem_spec),
         scratch_shapes=[
+            pltpu.SMEM((slabs,), F32),
             vmem((slabs, 2, size, size), F32),
             vmem((slabs, 2, size, size), F32),
-            vmem(tall.shape, F32),
+            vmem(woven.shape, F32),
             vmem((slabs, 2, 2 * size, 2 * size), BF16),
             vmem((slabs, 2, 2 * size, 2 * size), BF16),
             vmem((slabs, 2 * size, size), F32),
-            vmem((slabs, 2, size, size), F32),
             vmem((slabs, energies, 2, rows, size), F32),
             vmem((2, size, size), F32),
             vmem((slabs, energies, 2, rows, size), F32),
-            pltpu.SemaphoreType.DMA((3,)),
+            pltpu.SemaphoreType.DMA((4,)),
             pltpu.SemaphoreType.DMA((CHUNKS,)),
             pltpu.SemaphoreType.DMA((CHUNKS,)),
             pltpu.SemaphoreType.DMA((slabs, energies)),
             pltpu.SemaphoreType.DMA((slabs, energies)),
-            pltpu.SemaphoreType.DMA((slabs,)),
         ],
-        compiler_params=pltpu.CompilerParams(collective_id=0, has_side_effects=True),
-    )(retain, hopping, source, tall)
-    return greens, self_energy.reshape(screened.shape)
+        compiler_params=pltpu.CompilerParams(
+            collective_id=0, has_side_effects=True
+        ),
+    )(retain.reshape(slabs), hopping, source, woven)
+    greens, self_energy = pl.pallas_call(
+        write_out,
+        out_shape=(
+            jax.ShapeDtypeStruct(source.shape, F32),
+            jax.ShapeDtypeStruct(woven.shape, F32),
+        ),
+        in_specs=[vmem_spec, vmem_spec],
+        out_specs=(any_spec, any_spec),
+        scratch_shapes=[pltpu.SemaphoreType.DMA((2,))],
+        compiler_params=pltpu.CompilerParams(vmem_limit_bytes=4 << 20),
+    )(greens, self_energy)
+    return greens, (
+        self_energy.reshape(slabs, energies, rows, 2, size)
+        .transpose(0, 1, 3, 2, 4)
+        .reshape(screened.shape)
+    )
 
 
 def solution(mesh):

time: 27.8 us -> 21.4 us (0.77)
  local copies, waits for them, and re-layouts: 5.69 us -> 0 us
  Pallas kernels: 21.2 us -> 20.6 us
    reshape x2 -> x0, local copies, waits for them, and re-layouts: 3.69 us -> none  [the longest x1 1.86 us: body(): tall = screened.reshape(slabs, energies, 2, rows, size)]
    unnamed x4 -> x0, local copies, waits for them, and re-layouts: 2 us -> none
    pallas_call x1 -> x2, Pallas kernels: 21.2 us -> 20.6 us  [the longest x1 19.8 us: body(): pl.pallas_call(kernel, out_shape=(vmem((slabs, 2, size, size), F32), vmem...]
where the time goes in v2:
time: 21.4 us; the launch traced here: 21.3 us
  Pallas kernels  20.6 us (96%)
  between operations  0.64 us (3%)
    pallas_call x1, Pallas kernels, body(): pl.pallas_call(kernel, out_shape=(vmem((slabs, 2, size, size), F32), vmem...  19.8 us
    pallas_call x1, Pallas kernels, body(): pl.pallas_call(write_out, out_shape=(jax.ShapeDtypeStruct(source.shape, F...  0.81 us

profile of v2, /device:TPU:25, one launch (start us, length us, event | category | flops | bytes accessed | tf_op | source)
XLA Modules:
  0.0 21.3 jit_solution(17653433250350497100)
XLA Ops:
  0.6 19.8 %shard_map.59 = (f32[2,2,128,128]{3,2,1,0:T(8,128)S(1)}, f32[2,8,32,128]{3,2,1,0:T(8,128)S(1)}) custom-call(f32[2]{0:T(128)} %bitcast.12, f32[2,1,2,128,128]{4,3,2,1,0:T(8,128)} %hop_hbm.1, f32[2,1,2,128,128]{4,3,2,1,0:T(8,128)} %src_hbm.1, f32[2,8,32,128]{3,2,1,0:T(8,128)} %bitcast.11), custom_call_target="tpu_custom_call" | custom-call | tf_op jit(solution)/shard_map/pallas_call | solution.py:244
  20.5 0.8 %shard_map.60 = (f32[2,1,2,128,128]{4,3,2,1,0:T(8,128)}, f32[2,8,32,128]{3,2,1,0:T(8,128)}) custom-call(f32[2,2,128,128]{3,2,1,0:T(8,128)S(1)} %get-tuple-element.6.g, f32[2,8,32,128]{3,2,1,0:T(8,128)S(1)} %get-tuple-element.7.se), custom_call_target="tpu_custom_call" | custom-call | tf_op jit(solution)/shard_map/pallas_call | solution.py:270

commit v3 on v2

--- a/solution.py
+++ b/solution.py
@@ -10,7 +10,7 @@
 MESH = pl.DeviceIdType.MESH
 F32 = jnp.float32
 BF16 = jnp.bfloat16
-CHUNKS = 2
+CHUNKS = 4
 NN = (((1,), (0,)), ((), ()))
 NT = (((1,), (1,)), ((), ()))
 
@@ -40,14 +40,16 @@
 
 def kernel(
     retain_hbm, hop_hbm, src_hbm, scr_hbm, g, out_se,
-    retain, hop, src, scr, lefts, rights, bases, stage, entering, landed,
-    load_sem, chain_send, chain_recv, swap_send, swap_recv,
+    retain, hop, src, scr, lefts, rights, bases, stage, entering, landed, own_map, early,
+    load_sem, chain_send, chain_recv, swap_send, swap_recv, early_send, early_recv,
 ):
     slabs, _, size, _ = hop.shape
     energies, rows = stage.shape[1], stage.shape[3]
     space, energy = lax.axis_index("space"), lax.axis_index("energy")
     stages = lax.axis_size("space")
     piece = size // CHUNKS
+    relays = (space % 2 == 0) & (space > 0) & (space < stages - 1)
+    paired = (space % 2 == 1) & (space > 1)
 
     loads = [
         pltpu.make_async_copy(hop_hbm.at[:, 0], hop, load_sem.at[0]),
@@ -97,13 +99,23 @@
         )
         bases[j] = base
 
-    def chain(c):
+    def chain(c, relay=False):
         part = pl.ds(c * piece, piece)
         return pltpu.make_async_remote_copy(
-            src_ref=g.at[slabs - 1, :, part],
+            src_ref=entering.at[:, part] if relay else g.at[slabs - 1, :, part],
             dst_ref=entering.at[:, part],
             send_sem=chain_send.at[c],
             recv_sem=chain_recv.at[c],
+            device_id=(space + 1, energy),
+            device_id_type=MESH,
+        )
+
+    def ahead(i):
+        return pltpu.make_async_remote_copy(
+            src_ref=bases.at[slabs - 1] if i else own_map,
+            dst_ref=early.at[i],
+            send_sem=early_send.at[i],
+            recv_sem=early_recv.at[i],
             device_id=(space + 1, energy),
             device_id_type=MESH,
         )
@@ -119,6 +131,12 @@
             device_id_type=MESH,
         )
 
+    def keep(j, real, imag):
+        for ref, form in ((lefts, left_form), (rights, dagger_form)):
+            high, low = split(form(real, imag))
+            ref[j, 0] = high
+            ref[j, 1] = low
+
     def put(j, block):
         g[j, 0] = block[:size]
         g[j, 1] = block[size:]
@@ -155,14 +173,34 @@
             if j > 0:
                 both = product(step_lefts[j], split(jnp.concatenate([real, imag], 0)))
                 real, imag = both[:size], both[size:]
-            for ref, form in ((lefts, left_form), (rights, dagger_form)):
-                high, low = split(form(real, imag))
-                ref[j, 0] = high
-                ref[j, 1] = low
+            keep(j, real, imag)
+        own_map[...] = jnp.concatenate([real, imag], 0)
+
+        @pl.when(relays)
+        def _():
+            ahead(0).start()
+            ahead(1).start()
+
+        @pl.when(paired)
+        def _():
+            ahead(0).wait_recv()
+            ahead(1).wait_recv()
+            before = split(early[0])
+            for j in range(slabs):
+                left = lefts[j, 0], lefts[j, 1]
+                right = rights[j, 0], rights[j, 1]
+                bases[j] = sandwich(left, right, early[1, :size], early[1, size:]) + bases[j]
+                both = product(left, before)
+                keep(j, both[:size], both[size:])
 
         turned = []
         for c in range(CHUNKS):
             chain(c).wait_recv()
+
+            @pl.when(relays)
+            def _():
+                chain(c, True).start()
+
             lines = slice(c * piece, (c + 1) * piece)
             arrived = split(jnp.concatenate([entering[0, lines], entering[1, lines]], 1))
             turned.append(product(arrived, (rights[last, 0], rights[last, 1]), NT))
@@ -170,7 +208,7 @@
         inner = split(jnp.concatenate([turned[:, :size], turned[:, size:]], 0))
         put(last, product((lefts[last, 0], lefts[last, 1]), inner) + bases[last])
 
-        @pl.when(space < stages - 1)
+        @pl.when((space < stages - 1) & (space % 2 == 1))
         def _():
             for c in range(CHUNKS):
                 chain(c).start()
@@ -212,10 +250,17 @@
         for step in range(1, energies):
             swap(j, step).wait_send()
 
-    @pl.when(space < stages - 1)
+    @pl.when((space < stages - 1) & jnp.logical_not(relays))
     def _():
         for c in range(CHUNKS):
             chain(c).wait_send()
+
+    @pl.when(relays)
+    def _():
+        ahead(0).wait_send()
+        ahead(1).wait_send()
+        for c in range(CHUNKS):
+            chain(c, True).wait_send()
 
 
 def write_out(g, se, out_g, out_se, sems):
@@ -257,11 +302,15 @@
             vmem((slabs, energies, 2, rows, size), F32),
             vmem((2, size, size), F32),
             vmem((slabs, energies, 2, rows, size), F32),
+            vmem((2 * size, size), F32),
+            vmem((2, 2 * size, size), F32),
             pltpu.SemaphoreType.DMA((4,)),
             pltpu.SemaphoreType.DMA((CHUNKS,)),
             pltpu.SemaphoreType.DMA((CHUNKS,)),
             pltpu.SemaphoreType.DMA((slabs, energies)),
             pltpu.SemaphoreType.DMA((slabs, energies)),
+            pltpu.SemaphoreType.DMA((2,)),
+            pltpu.SemaphoreType.DMA((2,)),
         ],
         compiler_params=pltpu.CompilerParams(
             collective_id=0, has_side_effects=True

time: 21.4 us -> 19.9 us (0.930)
  Pallas kernels: 20.6 us -> 19.1 us
    pallas_call x1, Pallas kernels: 19.8 us -> 18.3 us  [body(): pl.pallas_call(kernel, out_shape=(vmem((slabs, 2, size, size), F32), vmem...]
where the time goes in v3:
time: 19.9 us; the launch traced here: 19.7 us
  Pallas kernels  19.1 us (96%)
  between operations  0.64 us (3%)
    pallas_call x1, Pallas kernels, body(): pl.pallas_call(kernel, out_shape=(vmem((slabs, 2, size, size), F32), vmem...  18.3 us
    pallas_call x1, Pallas kernels, body(): pl.pallas_call(write_out, out_shape=(jax.ShapeDtypeStruct(source.shape, F...  0.81 us

profile of v3, /device:TPU:25, one launch (start us, length us, event | category | flops | bytes accessed | tf_op | source)
XLA Modules:
  0.0 19.7 jit_solution(18123513504451992102)
XLA Ops:
  0.6 18.3 %shard_map.59 = (f32[2,2,128,128]{3,2,1,0:T(8,128)S(1)}, f32[2,8,32,128]{3,2,1,0:T(8,128)S(1)}) custom-call(f32[2]{0:T(128)} %bitcast.12, f32[2,1,2,128,128]{4,3,2,1,0:T(8,128)} %hop_hbm.1, f32[2,1,2,128,128]{4,3,2,1,0:T(8,128)} %src_hbm.1, f32[2,8,32,128]{3,2,1,0:T(8,128)} %bitcast.11), custom_call_target="tpu_custom_call" | custom-call | tf_op jit(solution)/shard_map/pallas_call | solution.py:289
  18.9 0.8 %shard_map.60 = (f32[2,1,2,128,128]{4,3,2,1,0:T(8,128)}, f32[2,8,32,128]{3,2,1,0:T(8,128)}) custom-call(f32[2,2,128,128]{3,2,1,0:T(8,128)S(1)} %get-tuple-element.6.g, f32[2,8,32,128]{3,2,1,0:T(8,128)S(1)} %get-tuple-element.7.se), custom_call_target="tpu_custom_call" | custom-call | tf_op jit(solution)/shard_map/pallas_call | solution.py:319

commit v4 on v3

--- a/solution.py
+++ b/solution.py
@@ -10,9 +10,10 @@
 MESH = pl.DeviceIdType.MESH
 F32 = jnp.float32
 BF16 = jnp.bfloat16
-CHUNKS = 4
+CHUNKS = 8
+GROUPS = 1
+OUTS = 2
 NN = (((1,), (0,)), ((), ()))
-NT = (((1,), (1,)), ((), ()))
 
 
 def split(value):
@@ -33,8 +34,9 @@
 
 
 def dagger_form(real, imag):
+    real, imag = real.T, imag.T
     return jnp.concatenate(
-        [jnp.concatenate([real, imag], 1), jnp.concatenate([-imag, real], 1)], 0
+        [jnp.concatenate([real, -imag], 1), jnp.concatenate([imag, real], 1)], 0
     )
 
 
@@ -84,7 +86,7 @@
         couplers.append((factor * (eye + hop[j, 0]), factor * hop[j, 1]))
 
     def sandwich(left, right, real, imag):
-        turned = product(split(jnp.concatenate([real, imag], 1)), right, NT)
+        turned = product(split(jnp.concatenate([real, imag], 1)), right)
         return product(left, split(jnp.concatenate([turned[:, :size], turned[:, size:]], 0)))
 
     base = jnp.concatenate([src[0, 0], src[0, 1]], 0)
@@ -201,17 +203,25 @@
             def _():
                 chain(c, True).start()
 
-            lines = slice(c * piece, (c + 1) * piece)
-            arrived = split(jnp.concatenate([entering[0, lines], entering[1, lines]], 1))
-            turned.append(product(arrived, (rights[last, 0], rights[last, 1]), NT))
+            if (c + 1) % (CHUNKS // GROUPS) == 0:
+                lines = slice((c + 1) * piece - size // GROUPS, (c + 1) * piece)
+                arrived = split(jnp.concatenate([entering[0, lines], entering[1, lines]], 1))
+                turned.append(product(arrived, (rights[last, 0], rights[last, 1])))
         turned = jnp.concatenate(turned, 0)
         inner = split(jnp.concatenate([turned[:, :size], turned[:, size:]], 0))
-        put(last, product((lefts[last, 0], lefts[last, 1]), inner) + bases[last])
-
-        @pl.when((space < stages - 1) & (space % 2 == 1))
-        def _():
-            for c in range(CHUNKS):
-                chain(c).start()
+        height = size // OUTS
+        for o in range(OUTS):
+            for part in range(2):
+                lines = slice(part * size + o * height, part * size + (o + 1) * height)
+                left = lefts[last, 0, lines], lefts[last, 1, lines]
+                g[last, part, o * height : (o + 1) * height] = (
+                    product(left, inner) + bases[last, lines]
+                )
+
+            @pl.when((space < stages - 1) & (space % 2 == 1))
+            def _():
+                for c in range(o * CHUNKS // OUTS, (o + 1) * CHUNKS // OUTS):
+                    chain(c).start()
 
         spread(last)
         for j in range(last - 1, -1, -1):

time: 19.9 us -> 19.7 us (0.990)
  Pallas kernels: 19.1 us -> 18.9 us
where the time goes in v4:
time: 19.7 us; the launch traced here: 19.5 us
  Pallas kernels  18.9 us (96%)
  between operations  0.64 us (3%)
    pallas_call x1, Pallas kernels, body(): pl.pallas_call(kernel, out_shape=(vmem((slabs, 2, size, size), F32), vmem...  18.1 us
    pallas_call x1, Pallas kernels, body(): pl.pallas_call(write_out, out_shape=(jax.ShapeDtypeStruct(source.shape, F...  0.81 us

profile of v4, /device:TPU:25, one launch (start us, length us, event | category | flops | bytes accessed | tf_op | source)
XLA Modules:
  0.0 19.5 jit_solution(7734565568223205826)
XLA Ops:
  0.6 18.1 %shard_map.59 = (f32[2,2,128,128]{3,2,1,0:T(8,128)S(1)}, f32[2,8,32,128]{3,2,1,0:T(8,128)S(1)}) custom-call(f32[2]{0:T(128)} %bitcast.12, f32[2,1,2,128,128]{4,3,2,1,0:T(8,128)} %hop_hbm.1, f32[2,1,2,128,128]{4,3,2,1,0:T(8,128)} %src_hbm.1, f32[2,8,32,128]{3,2,1,0:T(8,128)} %bitcast.11), custom_call_target="tpu_custom_call" | custom-call | tf_op jit(solution)/shard_map/pallas_call | solution.py:299
  18.7 0.8 %shard_map.60 = (f32[2,1,2,128,128]{4,3,2,1,0:T(8,128)}, f32[2,8,32,128]{3,2,1,0:T(8,128)}) custom-call(f32[2,2,128,128]{3,2,1,0:T(8,128)S(1)} %get-tuple-element.6.g, f32[2,8,32,128]{3,2,1,0:T(8,128)S(1)} %get-tuple-element.7.se), custom_call_target="tpu_custom_call" | custom-call | tf_op jit(solution)/shard_map/pallas_call | solution.py:329

commit v5 on v4

--- a/solution.py
+++ b/solution.py
@@ -24,7 +24,7 @@
 def product(left, right, dims=NN):
     dot = functools.partial(lax.dot_general, dimension_numbers=dims, preferred_element_type=F32)
     (lh, ll), (rh, rl) = left, right
-    return dot(lh, rh) + (dot(lh, rl) + dot(ll, rh))
+    return dot(jnp.concatenate([lh, lh, ll], 1), jnp.concatenate([rl, rh, rh], 0))
 
 
 def left_form(real, imag):
@@ -40,10 +40,24 @@
     )
 
 
+def round_count(energies):
+    return 0
+
+
+def near_peers(energy, energies):
+    if energies:
+        return [lax.rem(energy + step, energies) for step in range(1, energies)]
+    peers, width = [], 1
+    while width < energies:
+        peers.append(energy + width * (1 - 2 * ((energy // width) % 2)))
+        width *= 2
+    return peers
+
+
 def kernel(
     retain_hbm, hop_hbm, src_hbm, scr_hbm, g, out_se,
     retain, hop, src, scr, lefts, rights, bases, stage, entering, landed, own_map, early,
-    load_sem, chain_send, chain_recv, swap_send, swap_recv, early_send, early_recv,
+    load_sem, chain_send, chain_recv, swap_send, swap_recv, early_send, early_recv, ready,
 ):
     slabs, _, size, _ = hop.shape
     energies, rows = stage.shape[1], stage.shape[3]
@@ -63,10 +77,9 @@
         load.start()
 
     barrier = pltpu.get_barrier_semaphore()
-    for step in range(1, energies):
-        pl.semaphore_signal(
-            barrier, inc=1, device_id=(space, lax.rem(energy + step, energies)), device_id_type=MESH
-        )
+    near = near_peers(energy, energies)
+    for peer in near:
+        pl.semaphore_signal(barrier, inc=1, device_id=(space, peer), device_id_type=MESH)
 
     @pl.when(space > 0)
     def _():
@@ -150,24 +163,6 @@
         for step in range(1, energies):
             swap(j, step).start()
 
-    pl.semaphore_wait(barrier, energies - 1 + (space < stages - 1).astype(jnp.int32))
-
-    last = slabs - 1
-
-    @pl.when(space == 0)
-    def _():
-        put(last, bases[last])
-
-        @pl.when(space < stages - 1)
-        def _():
-            for c in range(CHUNKS):
-                chain(c).start()
-
-        spread(last)
-        for j in range(last - 1, -1, -1):
-            put(j, bases[j])
-            spread(j)
-
     @pl.when(space > 0)
     def _():
         real, imag = couplers[0]
@@ -178,11 +173,38 @@
             keep(j, real, imag)
         own_map[...] = jnp.concatenate([real, imag], 0)
 
-        @pl.when(relays)
+    pl.semaphore_wait(barrier, len(near) + (space < stages - 1).astype(jnp.int32))
+
+    last = slabs - 1
+
+    @pl.when(space == 0)
+    def _():
+        put(last, bases[last])
+
+        @pl.when(space < stages - 1)
         def _():
-            ahead(0).start()
-            ahead(1).start()
-
+            for c in range(CHUNKS):
+                chain(c).start()
+
+    @pl.when(relays)
+    def _():
+        ahead(0).start()
+        ahead(1).start()
+
+    for r in range(round_count(energies)):
+        for peer in near:
+            pl.semaphore_signal(ready.at[r], inc=1, device_id=(space, peer), device_id_type=MESH)
+        pl.semaphore_wait(ready.at[r], len(near))
+
+    @pl.when(space == 0)
+    def _():
+        spread(last)
+        for j in range(last - 1, -1, -1):
+            put(j, bases[j])
+            spread(j)
+
+    @pl.when(space > 0)
+    def _():
         @pl.when(paired)
         def _():
             ahead(0).wait_recv()
@@ -321,6 +343,7 @@
             pltpu.SemaphoreType.DMA((slabs, energies)),
             pltpu.SemaphoreType.DMA((2,)),
             pltpu.SemaphoreType.DMA((2,)),
+            pltpu.SemaphoreType.REGULAR((max(1, round_count(energies)),)),
         ],
         compiler_params=pltpu.CompilerParams(
             collective_id=0, has_side_effects=True

time: 19.7 us -> 19.7 us (level)
  no operation moved by 1% of the time
where the time goes in v5:
time: 19.7 us; the launch traced here: 19.5 us
  Pallas kernels  18.9 us (96%)
  between operations  0.64 us (3%)
    pallas_call x1, Pallas kernels, body(): pl.pallas_call(kernel, out_shape=(vmem((slabs, 2, size, size), F32), vmem...  18.1 us
    pallas_call x1, Pallas kernels, body(): pl.pallas_call(write_out, out_shape=(jax.ShapeDtypeStruct(source.shape, F...  0.81 us

profile of v5, /device:TPU:25, one launch (start us, length us, event | category | flops | bytes accessed | tf_op | source)
XLA Modules:
  0.0 19.5 jit_solution(14797376671803934003)
XLA Ops:
  0.6 18.1 %shard_map.59 = (f32[2,2,128,128]{3,2,1,0:T(8,128)S(1)}, f32[2,8,32,128]{3,2,1,0:T(8,128)S(1)}) custom-call(f32[2]{0:T(128)} %bitcast.12, f32[2,1,2,128,128]{4,3,2,1,0:T(8,128)} %hop_hbm.1, f32[2,1,2,128,128]{4,3,2,1,0:T(8,128)} %src_hbm.1, f32[2,8,32,128]{3,2,1,0:T(8,128)} %bitcast.11), custom_call_target="tpu_custom_call" | custom-call | tf_op jit(solution)/shard_map/pallas_call | solution.py:321
  18.7 0.8 %shard_map.60 = (f32[2,1,2,128,128]{4,3,2,1,0:T(8,128)}, f32[2,8,32,128]{3,2,1,0:T(8,128)}) custom-call(f32[2,2,128,128]{3,2,1,0:T(8,128)S(1)} %get-tuple-element.6.g, f32[2,8,32,128]{3,2,1,0:T(8,128)S(1)} %get-tuple-element.7.se), custom_call_target="tpu_custom_call" | custom-call | tf_op jit(solution)/shard_map/pallas_call | solution.py:352
